TPU v7x, 128 devices: a whole 4x4x4 slice. The times are simulated.
128 devices in a mesh: row: 64 (over z, y, x), pan: 2 (over core).
Axes of the slice: x: 4, y: 4, z: 4, core: 2. Of those that a mesh axis runs over, the one named last changes fastest.
Arguments:
- right_side: float32 [256, 65536], P(None, 'row'), may hold values from -6 to 6
- initial_guess: float32 [256, 65536], P(None, ('row', 'pan')), may hold values from -6 to 6
- v_factor: float32 [128, 128, 16, 512], P('row', None, 'pan'), may hold values from -0.25 to 0.25
- u_factor: float32 [128, 128, 16, 512], P('row', None, 'pan'), may hold values from -0.125 to 0.125
- tile_ranks: int32 [128, 128], P(None, 'row'), may hold values from 0 to 16
- diag_block: float32 [65536, 512], P(('row', 'pan'))
- diag_inverse: float32 [65536, 512], P(('row', 'pan'))
Outputs:
- solution: float32 [256, 65536], P(None, ('row', 'pan'))
- residual: float32 [256, 65536], P(None, ('row', 'pan'))
Inputs may be any that keep to these rules, and one draw needn't show every extreme that they name: `tile_ranks`: columns of a tile's factors from its rank on are ignored, as is the low-rank part of tile (i, i).
All inputs are finite; a program needn't handle non-finite values.
Results may differ from a plain program's by a relative error of at most 0.00017.
Values sent between devices are 32-bit elements; how exact they have to be, the bound alone decides.
A program may use at most 64 MiB of HBM per device.

v0:
```python
import jax
import jax.numpy as jnp
from jax import lax
from jax.sharding import PartitionSpec as P

ITERS = 2


def on_device(right_side, initial_guess, v_factor, u_factor, tile_ranks, diag_block, diag_inverse):
    highest = lax.Precision.HIGHEST
    pan_index = lax.axis_index("pan")
    row_index = lax.axis_index("row")
    tile_rows = v_factor.shape[0]
    tile_count = v_factor.shape[1]
    part_rank = v_factor.shape[2]
    tile_width = v_factor.shape[3]
    rhs_count = right_side.shape[0]
    own_rows = diag_block.shape[0]
    row_start = pan_index * own_rows
    tile_slot = row_start // tile_width
    components = pan_index * part_rank + jnp.arange(part_rank, dtype=jnp.int32)
    own_columns = row_index * tile_rows + jnp.arange(tile_rows, dtype=jnp.int32)
    tile_index = jnp.arange(tile_count, dtype=jnp.int32)
    off_diagonal = tile_index[:, None] != own_columns[None, :]
    rank_mask = (
        (components[None, None, :] < tile_ranks[:, :, None]) & off_diagonal[:, :, None]
    ).astype(jnp.float32)
    iterate_rows = initial_guess
    residual = initial_guess
    for iteration in range(ITERS):
        guess_full = lax.all_gather(iterate_rows, "pan", axis=1, tiled=True)
        guess_tiles = guess_full.reshape(rhs_count, tile_rows, tile_width)
        projected = jnp.einsum("cikb,rcb->ickr", v_factor, guess_tiles, precision=highest)
        projected = projected * rank_mask[:, :, :, None]
        received = lax.all_to_all(projected, "row", split_axis=0, concat_axis=1, tiled=True)
        low_rank = jnp.einsum("ickm,ickr->rim", u_factor, received, precision=highest)
        low_rank = low_rank.reshape(rhs_count, tile_rows * tile_width)
        guess_tile = lax.dynamic_slice_in_dim(guess_full, tile_slot * tile_width, tile_width, 1)
        dense_part = jnp.einsum("rb,mb->rm", guess_tile, diag_block, precision=highest)
        low_rows = lax.psum_scatter(low_rank, "pan", scatter_dimension=1, tiled=True)
        rhs_rows = lax.dynamic_slice_in_dim(right_side, row_start, own_rows, 1)
        residual = rhs_rows - (dense_part + low_rows)
        residual_full = lax.all_gather(residual, "pan", axis=1, tiled=True)
        residual_tile = lax.dynamic_slice_in_dim(
            residual_full, tile_slot * tile_width, tile_width, 1
        )
        update = jnp.einsum("rb,mb->rm", residual_tile, diag_inverse, precision=highest)
        iterate_rows = iterate_rows + update
    return (iterate_rows, residual)


def solution(mesh):
    placed = (
        P(None, "row"),
        P(None, ("row", "pan")),
        P("row", None, "pan", None),
        P("row", None, "pan", None),
        P(None, "row"),
        P(("row", "pan"), None),
        P(("row", "pan"), None),
    )
    return jax.shard_map(
        on_device,
        mesh=mesh,
        in_specs=placed,
        out_specs=(P(None, ("row", "pan")), P(None, ("row", "pan"))),
        check_vma=False,
    )
```

profile of v0, /device:TPU:1, one launch (start us, length us, event | category | flops | bytes accessed | tf_op | source)
XLA Modules:
  0.0 225.6 jit_solution(9807114171824869542)
XLA Ops:
  7.2 0.0 copy-start
  7.2 0.0 all-gather.5.cloned.1.call-start
  7.2 2.1 copy.33
  9.3 0.0 all-gather.5.cloned.1.call-update
  9.4 0.0 reduce-scatter.3.cloned.1.call-start
  9.4 0.1 iota_compare_fusion
  9.5 0.8 and_convert_fusion
  10.3 15.4 %all-gather.5.cloned.1.call-done = f32[256,1024]{0,1:T(8,128)} async-done(((f32[256,512]{0,1:T(8,128)}), f32[256,1024]{0,1:T(8,128)}) %all-gather.5.cloned.1.call-update) | async-done | bytes 1048592 | tf_op jit(solution)/shard_map/all_gather | solution.py:31
  25.7 12.3 %bitcast_multiply_fusion.1 = f32[128,2,8,256]{0,3,2,1:T(8,128)} fusion(f32[256,2,512,1]{0,2,3,1:T(8,128)} %bitcast.45, f32[2,128,8,512]{3,2,1,0:T(8,128)} %param.9, f32[128,2,8]{0,2,1:T(8,128)S(1)} %and_convert_fusion), kind=kOutput, calls=%fused_computation.5 | convolution fusion | flops 3221749760 | bytes 7348224 | tf_op jit(solution)/shard_map/cikb,rcb->ickr/dot_general | solution.py:33
  38.0 2.2 copy.36
  40.2 39.2 %all_to_all.36 = f32[128,2,8,256]{3,2,1,0:T(8,128)S(1)} all-to-all(f32[128,2,8,256]{3,2,1,0:T(8,128)S(1)} %copy.36), channel_id=1, replica_groups=mesh['row'=64,'pan'=2] {'row'}, dimensions={0} | all-to-all | bytes 4194304 | tf_op jit(solution)/shard_map/all_to_all | solution.py:35
  79.5 0.0 copy-start.5
  79.5 0.2 copy.37
  79.7 2.0 copy-done.5
  81.7 3.8 %convolution_bitcast_fusion.1 = f32[256,2,512]{2,0,1:T(8,128)S(1)} fusion(f32[2,128,8,256]{3,2,1,0:T(8,128)S(1)} %bitcast.46, f32[2,128,8,512]{3,2,1,0:T(8,128)S(1)} %copy-done.5), kind=kOutput, calls=%fused_computation.7 | convolution fusion | flops 3221225472 | bytes 7340032 | tf_op jit(solution)/shard_map/ickm,ickr->rim/dot_general | solution.py:36
  85.5 0.3 copy.38
  85.9 0.0 copy-start.4
  85.9 1.3 copy.39
  87.2 0.0 reduce-scatter.3.cloned.1.call-update
  87.2 0.0 copy-start.2
  87.2 0.0 all-gather.7.cloned.1.call-start
  87.3 9.3 %reduce-scatter.3.cloned.1.call-done = f32[256,512]{1,0:T(8,128)} async-done(((f32[256,1024]{1,0:T(8,128)}), f32[256,512]{1,0:T(8,128)}) %reduce-scatter.3.cloned.1.call-update) | async-done | bytes 524304 | tf_op jit(solution)/shard_map/reduce_scatter | solution.py:40
  96.6 0.0 copy-done
  96.6 0.0 copy-done.4
  96.6 3.9 %fusion.8 = f32[256,512]{1,0:T(8,128)} fusion(f32[256,512]{1,0:T(8,128)} %reduce-scatter.3.cloned.1.call-done, f32[512,512]{1,0:T(8,128)S(1)} %copy-done, f32[256,1024]{0,1:T(8,128)S(1)} %copy-done.4, s32[]{:T(128)S(6)} %select_n.17, f32[256,1024]{1,0:T(8,128)} %param.7, s32[]{:T(128)S(6)} %select_n.15), kind=kOutput, calls=%fused_computation.12 | convolution fusion | flops 805568512 | bytes 3145736 | tf_op jit(solution)/shard_map/rb,mb->rm/dot_general | solution.py:39
  100.5 0.0 all-gather.7.cloned.1.call-update
  100.5 0.0 all-gather.9.cloned.1.call-start
  100.6 13.2 %all-gather.7.cloned.1.call-done = f32[256,1024]{1,0:T(8,128)} async-done(((f32[256,512]{1,0:T(8,128)}), f32[256,1024]{1,0:T(8,128)}) %all-gather.7.cloned.1.call-update) | async-done | bytes 1048592 | tf_op jit(solution)/shard_map/all_gather | solution.py:43
  113.7 0.0 copy-done.2
  113.7 3.1 %convolution_add_fusion.2 = f32[256,512]{1,0:T(8,128)} fusion(f32[256,512]{1,0:T(8,128)} %param.8, f32[512,512]{1,0:T(8,128)S(1)} %copy-done.2, f32[256,1024]{1,0:T(8,128)} %all-gather.7.cloned.1.call-done, s32[]{:T(128)S(6)} %select_n.17), kind=kOutput, calls=%fused_computation.10 | convolution fusion | flops 805437440 | bytes 2621444 | tf_op jit(solution)/shard_map/rb,mb->rm/dot_general | solution.py:47
  116.8 0.0 all-gather.9.cloned.1.call-update
  116.8 0.3 reduce-scatter.5.cloned.1.call-start
  117.1 13.0 %all-gather.9.cloned.1.call-done = f32[256,1024]{1,0:T(8,128)} async-done(((f32[256,512]{1,0:T(8,128)}), f32[256,1024]{1,0:T(8,128)}) %all-gather.9.cloned.1.call-update) | async-done | bytes 1048592 | tf_op jit(solution)/shard_map/all_gather | solution.py:31
  130.0 2.1 reshape.49
  132.1 9.3 %bitcast_multiply_fusion = f32[128,2,8,256]{0,3,2,1:T(8,128)} fusion(f32[2,128,8,512]{3,2,1,0:T(8,128)} %param.9, f32[256,2,512,1]{2,1,0,3:T(2,128)S(1)} %bitcast.44, f32[128,2,8]{0,2,1:T(8,128)S(1)} %and_convert_fusion), kind=kOutput, calls=%fused_computation.4 | convolution fusion | flops 3221749760 | bytes 7348224 | tf_op jit(solution)/shard_map/cikb,rcb->ickr/dot_general | solution.py:33
  141.4 2.2 copy.42
  143.7 39.2 %all_to_all.37 = f32[128,2,8,256]{3,2,1,0:T(8,128)S(1)} all-to-all(f32[128,2,8,256]{3,2,1,0:T(8,128)S(1)} %copy.42), channel_id=1, replica_groups=mesh['row'=64,'pan'=2] {'row'}, dimensions={0} | all-to-all | bytes 4194304 | tf_op jit(solution)/shard_map/all_to_all | solution.py:35
  182.9 0.0 copy-start.6
  182.9 0.2 copy.43
  183.1 2.0 copy-done.6
  185.1 3.8 %convolution_bitcast_fusion = f32[2,32,8,512]{3,2,1,0:T(8,128)S(1)} fusion(f32[2,128,8,256]{3,2,1,0:T(8,128)S(1)} %bitcast.47, f32[2,128,8,512]{3,2,1,0:T(8,128)S(1)} %copy-done.6), kind=kOutput, calls=%fused_computation.6 | convolution fusion | flops 3221225472 | bytes 7340032 | tf_op jit(solution)/shard_map/ickm,ickr->rim/dot_general | solution.py:36
  188.9 1.1 copy.53
  190.0 0.0 reduce-scatter.5.cloned.1.call-update
  190.0 0.0 copy-start.1
  190.1 0.0 copy-start.3
  190.1 0.0 all-gather.11.cloned.1.call-start
  190.1 9.3 %reduce-scatter.5.cloned.1.call-done = f32[256,512]{1,0:T(8,128)} async-done(((f32[256,1024]{1,0:T(8,128)}), f32[256,512]{1,0:T(8,128)}) %reduce-scatter.5.cloned.1.call-update) | async-done | bytes 524304 | tf_op jit(solution)/shard_map/reduce_scatter | solution.py:40
  199.5 3.2 %fusion.9 = f32[256,512]{1,0:T(8,128)} fusion(f32[256,512]{1,0:T(8,128)} %reduce-scatter.5.cloned.1.call-done, f32[512,512]{1,0:T(8,128)S(1)} %copy-done, f32[256,1024]{1,0:T(8,128)} %all-gather.9.cloned.1.call-done, s32[]{:T(128)S(6)} %select_n.17, f32[256,1024]{1,0:T(8,128)} %param.7, s32[]{:T(128)S(6)} %select_n.15), kind=kOutput, calls=%fused_computation.13 | convolution fusion | flops 805568512 | bytes 3145736 | tf_op jit(solution)/shard_map/rb,mb->rm/dot_general | solution.py:39
  202.7 0.0 all-gather.11.cloned.1.call-update
  202.7 13.2 %all-gather.11.cloned.1.call-done = f32[256,1024]{1,0:T(8,128)} async-done(((f32[256,512]{1,0:T(8,128)}), f32[256,1024]{1,0:T(8,128)}) %all-gather.11.cloned.1.call-update) | async-done | bytes 1048592 | tf_op jit(solution)/shard_map/all_gather | solution.py:43
  215.9 0.0 copy-done.1
  215.9 0.0 copy-done.3
  215.9 2.9 %convolution_add_fusion = f32[256,512]{1,0:T(8,128)} fusion(f32[256,512]{1,0:T(8,128)S(1)} %copy-done.1, f32[512,512]{1,0:T(8,128)S(1)} %copy-done.3, f32[256,1024]{1,0:T(8,128)} %all-gather.11.cloned.1.call-done, s32[]{:T(128)S(6)} %select_n.17), kind=kOutput, calls=%fused_computation.8 | convolution fusion | flops 805437440 | bytes 2621444 | tf_op jit(solution)/shard_map/rb,mb->rm/dot_general | solution.py:47
  (2 shorter events, 0.0 us)
Async XLA Ops:
  7.2 89.5 %copy-start = (f32[512,512]{1,0:T(8,128)S(1)}, f32[512,512]{1,0:T(8,128)}, u32[]{:S(2)}) copy-start(f32[512,512]{1,0:T(8,128)} %param.12) | copy-start | bytes 3145732
  7.2 18.5 %all-gather.5.cloned.1.call-start = ((), (), s32[]{:S(2)}) async-start(), calls=%async_computation.4 | async-start | bytes 1572864 | tf_op jit(solution)/shard_map/all_gather | solution.py:31
  9.4 87.3 %reduce-scatter.3.cloned.1.call-start = ((), (), s32[]{:S(2)}) async-start(), calls=%async_computation.5 | async-start | bytes 1572864 | tf_op jit(solution)/shard_map/reduce_scatter | solution.py:40
  79.5 2.2 copy-start.5
  85.9 10.8 %copy-start.4 = (f32[256,1024]{0,1:T(8,128)S(1)}, f32[256,1024]{0,1:T(8,128)}, u32[]{:S(2)}) copy-start(f32[256,1024]{0,1:T(8,128)} %all-gather.5.cloned.1.call-done) | copy-start | bytes 3145732
  87.2 26.5 %copy-start.2 = (f32[512,512]{1,0:T(8,128)S(1)}, f32[512,512]{1,0:T(8,128)}, u32[]{:S(2)}) copy-start(f32[512,512]{1,0:T(8,128)} %param.13) | copy-start | bytes 3145732
  87.2 26.5 %all-gather.7.cloned.1.call-start = ((), (), s32[]{:S(2)}) async-start(), calls=%async_computation.6 | async-start | bytes 1572864 | tf_op jit(solution)/shard_map/all_gather | solution.py:43
  100.5 29.5 %all-gather.9.cloned.1.call-start = ((), (), s32[]{:S(2)}) async-start(), calls=%async_computation.7 | async-start | bytes 1572864 | tf_op jit(solution)/shard_map/all_gather | solution.py:31
  116.8 82.6 %reduce-scatter.5.cloned.1.call-start = ((), (), s32[]{:S(2)}) async-start(), calls=%async_computation.8 | async-start | bytes 1572864 | tf_op jit(solution)/shard_map/reduce_scatter | solution.py:40
  182.9 2.2 copy-start.6
  190.0 25.9 %copy-start.1 = (f32[256,512]{1,0:T(8,128)S(1)}, f32[256,512]{1,0:T(8,128)}, u32[]{:S(2)}) copy-start(f32[256,512]{1,0:T(8,128)} %convolution_add_fusion.2) | copy-start | bytes 1572868
  190.1 25.9 %copy-start.3 = (f32[512,512]{1,0:T(8,128)S(1)}, f32[512,512]{1,0:T(8,128)}, u32[]{:S(2)}) copy-start(f32[512,512]{1,0:T(8,128)} %param.13) | copy-start | bytes 3145732
  190.1 25.8 %all-gather.11.cloned.1.call-start = ((), (), s32[]{:S(2)}) async-start(), calls=%async_computation.9 | async-start | bytes 1572864 | tf_op jit(solution)/shard_map/all_gather | solution.py:43
Sparse Core Ops, SparseCore 0:
  10.2 15.3 all-gather.4
  87.3 9.2 reduce-scatter.2
  100.6 13.0 all-gather.6
  116.9 13.0 all-gather.8
  190.2 9.2 reduce-scatter.4
  202.8 13.0 all-gather.10
where the time goes:
time: 226 us
  blocking collectives  78.5 us (35%)
  waiting for transfers between devices  73.5 us (33%)
  matrix products  42.3 us (19%)
  local copies, waits for them, and re-layouts  15.8 us (7%)
  between operations  14.3 us (6%)
    all_to_all x2, blocking collectives, on_device(): lax.all_to_all(projected, 'row', split_axis=0, concat_axis=1, tiled=True)  78.5 us
    all_gather x2, waiting for transfers between devices, on_device(): guess_full = lax.all_gather(iterate_rows, 'pan', axis=1, tiled=True)  28.3 us
    all_gather x2, waiting for transfers between devices, on_device(): residual_full = lax.all_gather(residual, 'pan', axis=1, tiled=True)  26.4 us
    dot_general x2, matrix products, on_device(): jnp.einsum('cikb,rcb->ickr', v_factor, guess_tiles, precision=highest)  21.6 us
    reduce_scatter x2, waiting for transfers between devices, on_device(): lax.psum_scatter(low_rank, 'pan', scatter_dimension=1, tiled=True)  18.7 us
    dot_general x2, matrix products, on_device(): jnp.einsum('ickm,ickr->rim', u_factor, received, precision=highest)  7.64 us
    dot_general x2, matrix products, on_device(): jnp.einsum('rb,mb->rm', guess_tile, diag_block, precision=highest)  7.07 us
    unnamed x15, local copies, waits for them, and re-layouts  6.15 us
  transfers between devices with their start and end apart: 6, of which 6 were waited for; matrix products, arithmetic and copies ran while one was open for 0% of the time, Pallas kernels for 0%

commit v1 on v0

--- a/solution.py
+++ b/solution.py
@@ -40,7 +40,9 @@
         low_rows = lax.psum_scatter(low_rank, "pan", scatter_dimension=1, tiled=True)
         rhs_rows = lax.dynamic_slice_in_dim(right_side, row_start, own_rows, 1)
         residual = rhs_rows - (dense_part + low_rows)
-        residual_full = lax.all_gather(residual, "pan", axis=1, tiled=True)
+        residual_full = jnp.concatenate(
+            lax.all_to_all(jnp.stack([residual] * lax.axis_size("pan")), "pan", 0, 0), axis=1
+        )
         residual_tile = lax.dynamic_slice_in_dim(
             residual_full, tile_slot * tile_width, tile_width, 1
         )

time: 226 us -> 213 us (0.942)
  waiting for transfers between devices: 73.5 us -> 47.4 us
  blocking collectives: 78.5 us -> 88.1 us
  local copies, waits for them, and re-layouts: 15.8 us -> 19.1 us
    all_gather x2 -> x0, waiting for transfers between devices: 26.4 us -> none  [on_device(): residual_full = lax.all_gather(residual, 'pan', axis=1, tiled=True)]
    all_to_all x0 -> x2, blocking collectives: none -> 9.65 us  [on_device(): lax.all_to_all(jnp.stack([residual] * lax.axis_size('pan')), 'pan', 0, 0)]
    reshape x0 -> x2, local copies, waits for them, and re-layouts: none -> 3.86 us  [on_device(): jnp.concatenate(lax.all_to_all(jnp.stack([residual] * lax.axis_size('pan'...]
    unnamed x15 -> x21, local copies, waits for them, and re-layouts: 6.15 us -> 6.17 us
  transfers between devices with their start and end apart: 6 -> 4, of which waited for: 6 -> 4; matrix products, arithmetic and copies ran while one was open for 0% -> 0% of each run, Pallas kernels for 0% -> 0%
where the time goes in v1:
time: 213 us; the launch traced here: 212 us
  blocking collectives  88.1 us (41%)
  waiting for transfers between devices  47.4 us (22%)
  matrix products  42 us (20%)
  local copies, waits for them, and re-layouts  19.1 us (9%)
  between operations  14 us (7%)
    all_to_all x2, blocking collectives, on_device(): lax.all_to_all(projected, 'row', split_axis=0, concat_axis=1, tiled=True)  78.5 us
    all_gather x2, waiting for transfers between devices, on_device(): guess_full = lax.all_gather(iterate_rows, 'pan', axis=1, tiled=True)  28.6 us
    dot_general x2, matrix products, on_device(): jnp.einsum('cikb,rcb->ickr', v_factor, guess_tiles, precision=highest)  21.6 us
    reduce_scatter x2, waiting for transfers between devices, on_device(): lax.psum_scatter(low_rank, 'pan', scatter_dimension=1, tiled=True)  18.8 us
    all_to_all x2, blocking collectives, on_device(): lax.all_to_all(jnp.stack([residual] * lax.axis_size('pan')), 'pan', 0, 0)  9.65 us
    dot_general x2, matrix products, on_device(): jnp.einsum('ickm,ickr->rim', u_factor, received, precision=highest)  7.65 us
    dot_general x2, matrix products, on_device(): jnp.einsum('rb,mb->rm', residual_tile, diag_inverse, precision=highest)  7.57 us
    unnamed x21, local copies, waits for them, and re-layouts  6.17 us
  transfers between devices with their start and end apart: 4, of which 4 were waited for; matrix products, arithmetic and copies ran while one was open for 0% of the time, Pallas kernels for 0%

profile of v1, /device:TPU:1, one launch (start us, length us, event | category | flops | bytes accessed | tf_op | source)
XLA Modules:
  0.0 212.1 jit_solution(2231467667311967014)
XLA Ops:
  7.2 0.0 copy-start
  7.2 0.0 all-gather.3.cloned.1.call-start
  7.2 2.1 copy.35
  9.3 0.0 all-gather.3.cloned.1.call-update
  9.4 0.0 reduce-scatter.3.cloned.1.call-start
  9.4 0.1 iota_compare_fusion
  9.5 0.8 and_convert_fusion
  10.3 15.4 %all-gather.3.cloned.1.call-done = f32[256,1024]{0,1:T(8,128)} async-done(((f32[256,512]{0,1:T(8,128)}), f32[256,1024]{0,1:T(8,128)}) %all-gather.3.cloned.1.call-update) | async-done | bytes 1048592 | tf_op jit(solution)/shard_map/all_gather | solution.py:31
  25.7 12.3 %bitcast_multiply_fusion.1 = f32[128,2,8,256]{0,3,2,1:T(8,128)} fusion(f32[256,2,512,1]{0,2,3,1:T(8,128)} %bitcast.57, f32[2,128,8,512]{3,2,1,0:T(8,128)} %param.9, f32[128,2,8]{0,2,1:T(8,128)S(1)} %and_convert_fusion), kind=kOutput, calls=%fused_computation.5 | convolution fusion | flops 3221749760 | bytes 7348224 | tf_op jit(solution)/shard_map/cikb,rcb->ickr/dot_general | solution.py:33
  38.0 2.2 %copy.38 = f32[128,2,8,256]{3,2,1,0:T(8,128)S(1)} copy(f32[128,2,8,256]{0,3,2,1:T(8,128)} %bitcast_multiply_fusion.1) | data formatting | bytes 4194304 | tf_op jit(solution)/shard_map/mul | solution.py:34
  40.2 39.2 %all_to_all.46 = f32[128,2,8,256]{3,2,1,0:T(8,128)S(1)} all-to-all(f32[128,2,8,256]{3,2,1,0:T(8,128)S(1)} %copy.38), channel_id=1, replica_groups=mesh['row'=64,'pan'=2] {'row'}, dimensions={0} | all-to-all | bytes 4194304 | tf_op jit(solution)/shard_map/all_to_all | solution.py:35
  79.5 0.0 copy-start.8
  79.5 0.2 copy.39
  79.7 2.0 copy-done.8
  81.7 3.8 %convolution_bitcast_fusion.1 = f32[2,32,8,512]{3,2,1,0:T(8,128)S(1)} fusion(f32[2,128,8,256]{3,2,1,0:T(8,128)S(1)} %bitcast.58, f32[2,128,8,512]{3,2,1,0:T(8,128)S(1)} %copy-done.8), kind=kOutput, calls=%fused_computation.7 | convolution fusion | flops 3221225472 | bytes 7340032 | tf_op jit(solution)/shard_map/ickm,ickr->rim/dot_general | solution.py:36
  85.5 0.0 copy-start.5
  85.5 0.0 copy-start.7
  85.5 1.1 copy.56
  86.6 0.0 reduce-scatter.3.cloned.1.call-update
  86.6 0.0 all-gather.5.cloned.1.call-start
  86.7 9.3 %reduce-scatter.3.cloned.1.call-done = f32[256,512]{1,0:T(8,128)} async-done(((f32[256,1024]{1,0:T(8,128)}), f32[256,512]{1,0:T(8,128)}) %reduce-scatter.3.cloned.1.call-update) | async-done | bytes 524304 | tf_op jit(solution)/shard_map/reduce_scatter | solution.py:40
  96.0 0.0 copy-done
  96.0 0.0 copy-done.5
  96.0 0.0 copy-done.7
  96.0 2.9 %fusion.9 = f32[1,256,512]{2,1,0:T(8,128)S(1)} fusion(f32[256,512]{1,0:T(8,128)} %reduce-scatter.3.cloned.1.call-done, f32[512,512]{1,0:T(8,128)S(1)} %copy-done, f32[256,1024]{0,1:T(8,128)S(1)} %copy-done.5, s32[]{:T(128)S(6)} %select_n.17, f32[256,1024]{1,0:T(8,128)S(1)} %copy-done.7, s32[]{:T(128)S(6)} %select_n.15), kind=kOutput, calls=%fused_computation.13 | convolution fusion | flops 805568512 | bytes 3145736 | tf_op jit(solution)/shard_map/rb,mb->rm/dot_general | solution.py:39
  99.0 0.1 pad_maximum_fusion
  99.1 0.0 copy-start.2
  99.1 4.4 %all_to_all.47 = f32[2,256,512]{2,1,0:T(8,128)S(1)} all-to-all(f32[2,256,512]{2,1,0:T(8,128)S(1)} %pad_maximum_fusion), channel_id=1, replica_groups=mesh['row'=64,'pan'=2] {'pan'}, dimensions={0} | all-to-all | bytes 2097152 | tf_op jit(solution)/shard_map/all_to_all | solution.py:44
  103.5 1.3 copy.41
  104.8 0.0 copy-done.2
  104.8 3.9 %convolution_add_fusion.2 = f32[256,512]{1,0:T(8,128)} fusion(f32[256,512]{1,0:T(8,128)} %param.8, f32[512,512]{1,0:T(8,128)S(1)} %copy-done.2, f32[256,1024]{0,1:T(8,128)} %bitcast.56, s32[]{:T(128)S(6)} %select_n.17), kind=kOutput, calls=%fused_computation.10 | convolution fusion | flops 805437440 | bytes 2621444 | tf_op jit(solution)/shard_map/rb,mb->rm/dot_general | solution.py:49
  108.7 0.0 all-gather.5.cloned.1.call-update
  108.7 0.3 reduce-scatter.5.cloned.1.call-start
  109.0 13.2 %all-gather.5.cloned.1.call-done = f32[256,1024]{1,0:T(8,128)} async-done(((f32[256,512]{1,0:T(8,128)}), f32[256,1024]{1,0:T(8,128)}) %all-gather.5.cloned.1.call-update) | async-done | bytes 1048592 | tf_op jit(solution)/shard_map/all_gather | solution.py:31
  122.2 2.1 reshape.63
  124.3 9.3 %bitcast_multiply_fusion = f32[128,2,8,256]{0,3,2,1:T(8,128)} fusion(f32[2,128,8,512]{3,2,1,0:T(8,128)} %param.9, f32[256,2,512,1]{2,1,0,3:T(2,128)S(1)} %bitcast.54, f32[128,2,8]{0,2,1:T(8,128)S(1)} %and_convert_fusion), kind=kOutput, calls=%fused_computation.4 | convolution fusion | flops 3221749760 | bytes 7348224 | tf_op jit(solution)/shard_map/cikb,rcb->ickr/dot_general | solution.py:33
  133.6 2.2 %copy.44 = f32[128,2,8,256]{3,2,1,0:T(8,128)S(1)} copy(f32[128,2,8,256]{0,3,2,1:T(8,128)} %bitcast_multiply_fusion) | data formatting | bytes 4194304 | tf_op jit(solution)/shard_map/mul | solution.py:34
  135.9 39.3 %all_to_all.48 = f32[128,2,8,256]{3,2,1,0:T(8,128)S(1)} all-to-all(f32[128,2,8,256]{3,2,1,0:T(8,128)S(1)} %copy.44), channel_id=1, replica_groups=mesh['row'=64,'pan'=2] {'row'}, dimensions={0} | all-to-all | bytes 4194304 | tf_op jit(solution)/shard_map/all_to_all | solution.py:35
  175.1 0.0 copy-start.9
  175.1 0.2 copy.45
  175.3 2.0 copy-done.9
  177.3 3.8 %convolution_bitcast_fusion = f32[2,32,8,512]{3,2,1,0:T(8,128)S(1)} fusion(f32[2,128,8,256]{3,2,1,0:T(8,128)S(1)} %bitcast.59, f32[2,128,8,512]{3,2,1,0:T(8,128)S(1)} %copy-done.9), kind=kOutput, calls=%fused_computation.6 | convolution fusion | flops 3221225472 | bytes 7340032 | tf_op jit(solution)/shard_map/ickm,ickr->rim/dot_general | solution.py:36
  181.2 0.0 copy-start.4
  181.2 1.1 copy.57
  182.2 0.0 reduce-scatter.5.cloned.1.call-update
  182.3 9.4 %reduce-scatter.5.cloned.1.call-done = f32[256,512]{1,0:T(8,128)} async-done(((f32[256,1024]{1,0:T(8,128)}), f32[256,512]{1,0:T(8,128)}) %reduce-scatter.5.cloned.1.call-update) | async-done | bytes 524304 | tf_op jit(solution)/shard_map/reduce_scatter | solution.py:40
  191.7 0.0 copy-done.4
  191.7 2.3 %fusion.10 = f32[256,512]{1,0:T(8,128)S(1)} fusion(f32[256,512]{1,0:T(8,128)} %reduce-scatter.5.cloned.1.call-done, f32[512,512]{1,0:T(8,128)S(1)} %copy-done, f32[256,1024]{1,0:T(8,128)S(1)} %copy-done.4, s32[]{:T(128)S(6)} %select_n.17, f32[256,1024]{1,0:T(8,128)} %param.7, s32[]{:T(128)S(6)} %select_n.15), kind=kOutput, calls=%fused_computation.14 | convolution fusion | flops 805568512 | bytes 3145736 | tf_op jit(solution)/shard_map/rb,mb->rm/dot_general | solution.py:39
  193.9 0.0 copy-start.6
  193.9 0.1 pad_maximum_fusion.1
  194.1 0.0 copy-start.1
  194.1 0.0 copy-start.3
  194.1 5.2 %all_to_all.49 = f32[2,256,512]{2,1,0:T(8,128)} all-to-all(f32[2,256,512]{2,1,0:T(8,128)S(1)} %pad_maximum_fusion.1), channel_id=1, replica_groups=mesh['row'=64,'pan'=2] {'pan'}, dimensions={0} | all-to-all | bytes 2097152 | tf_op jit(solution)/shard_map/all_to_all | solution.py:44
  199.3 2.5 %copy.47 = f32[256,2,512]{0,2,1:T(8,128)} copy(f32[256,2,512]{2,0,1:T(8,128)} %bitcast.53) | data formatting | bytes 2097152 | tf_op jit(solution)/shard_map/reshape | solution.py:43
  201.9 0.0 copy-done.6
  201.9 0.0 copy-done.1
  201.9 0.0 copy-done.3
  201.9 3.7 %convolution_add_fusion = f32[256,512]{1,0:T(8,128)} fusion(f32[256,512]{1,0:T(8,128)S(1)} %copy-done.1, f32[512,512]{1,0:T(8,128)S(1)} %copy-done.3, f32[256,1024]{0,1:T(8,128)} %bitcast.55, s32[]{:T(128)S(6)} %select_n.17), kind=kOutput, calls=%fused_computation.8 | convolution fusion | flops 805437440 | bytes 2621444 | tf_op jit(solution)/shard_map/rb,mb->rm/dot_general | solution.py:49
  (2 shorter events, 0.0 us)
Async XLA Ops:
  7.2 88.9 %copy-start = (f32[512,512]{1,0:T(8,128)S(1)}, f32[512,512]{1,0:T(8,128)}, u32[]{:S(2)}) copy-start(f32[512,512]{1,0:T(8,128)} %param.12) | copy-start | bytes 3145732
  7.2 18.5 %all-gather.3.cloned.1.call-start = ((), (), s32[]{:S(2)}) async-start(), calls=%async_computation.6 | async-start | bytes 1572864 | tf_op jit(solution)/shard_map/all_gather | solution.py:31
  9.4 86.7 %reduce-scatter.3.cloned.1.call-start = ((), (), s32[]{:S(2)}) async-start(), calls=%async_computation.7 | async-start | bytes 1572864 | tf_op jit(solution)/shard_map/reduce_scatter | solution.py:40
  79.5 2.2 %copy-start.8 = (f32[2,128,8,512]{3,2,1,0:T(8,128)S(1)}, f32[2,128,8,512]{3,2,1,0:T(8,128)}, u32[]{:S(2)}) copy-start(f32[2,128,8,512]{3,2,1,0:T(8,128)} %param.10) | copy-start | bytes 12582916
  85.5 10.5 %copy-start.5 = (f32[256,1024]{0,1:T(8,128)S(1)}, f32[256,1024]{0,1:T(8,128)}, u32[]{:S(2)}) copy-start(f32[256,1024]{0,1:T(8,128)} %all-gather.3.cloned.1.call-done) | copy-start | bytes 3145732
  85.5 10.5 %copy-start.7 = (f32[256,1024]{1,0:T(8,128)S(1)}, f32[256,1024]{1,0:T(8,128)}, u32[]{:S(2)}) copy-start(f32[256,1024]{1,0:T(8,128)} %param.7) | copy-start | bytes 3145732
  86.6 35.6 %all-gather.5.cloned.1.call-start = ((), (), s32[]{:S(2)}) async-start(), calls=%async_computation.8 | async-start | bytes 1572864 | tf_op jit(solution)/shard_map/all_gather | solution.py:31
  99.1 5.7 %copy-start.2 = (f32[512,512]{1,0:T(8,128)S(1)}, f32[512,512]{1,0:T(8,128)}, u32[]{:S(2)}) copy-start(f32[512,512]{1,0:T(8,128)} %param.13) | copy-start | bytes 3145732
  108.7 82.9 %reduce-scatter.5.cloned.1.call-start = ((), (), s32[]{:S(2)}) async-start(), calls=%async_computation.9 | async-start | bytes 1572864 | tf_op jit(solution)/shard_map/reduce_scatter | solution.py:40
  175.1 2.2 %copy-start.9 = (f32[2,128,8,512]{3,2,1,0:T(8,128)S(1)}, f32[2,128,8,512]{3,2,1,0:T(8,128)}, u32[]{:S(2)}) copy-start(f32[2,128,8,512]{3,2,1,0:T(8,128)} %param.10) | copy-start | bytes 12582916
  181.2 10.5 %copy-start.4 = (f32[256,1024]{1,0:T(8,128)S(1)}, f32[256,1024]{1,0:T(8,128)}, u32[]{:S(2)}) copy-start(f32[256,1024]{1,0:T(8,128)} %all-gather.5.cloned.1.call-done) | copy-start | bytes 3145732
  193.9 7.9 %copy-start.6 = (f32[256,512]{1,0:T(8,128)}, f32[256,512]{1,0:T(8,128)S(1)}, u32[]{:S(2)}) copy-start(f32[256,512]{1,0:T(8,128)S(1)} %fusion.10) | copy-start | bytes 1572868
  194.1 7.8 %copy-start.1 = (f32[256,512]{1,0:T(8,128)S(1)}, f32[256,512]{1,0:T(8,128)}, u32[]{:S(2)}) copy-start(f32[256,512]{1,0:T(8,128)} %convolution_add_fusion.2) | copy-start | bytes 1572868
  194.1 7.8 %copy-start.3 = (f32[512,512]{1,0:T(8,128)S(1)}, f32[512,512]{1,0:T(8,128)}, u32[]{:S(2)}) copy-start(f32[512,512]{1,0:T(8,128)} %param.13) | copy-start | bytes 3145732
Sparse Core Ops, SparseCore 0:
  10.2 15.3 all-gather.2
  86.7 9.2 reduce-scatter.2
  108.8 13.3 all-gather.4
  182.4 9.2 reduce-scatter.4
